TPU v7x, 32 devices: a whole 2x2x4 slice. The times are simulated.
32 devices in a mesh: groups: 2 (over x), frame: 16 (over z, y, core).
Axes of the slice: x: 2, y: 2, z: 4, core: 2. Of those that a mesh axis runs over, the one named last changes fastest.
Arguments:
- queries: bfloat16 [4096, 2048], P(('groups', 'frame')), parts along dimension 0, may hold values from -40 to 40, as said below
- key_rows: bfloat16 [4096, 2048], P(('groups', 'frame')), parts along dimension 0, may hold values from -4 to 4
- value_rows: bfloat16 [4096, 2048], P(('groups', 'frame')), parts along dimension 0, may hold values from -6 to 6
- slopes: bfloat16 [16], replicated, may hold values from 0.0019989014 to 0.19921875
- noise_level: int32 [32], P('groups'), parts along dimension 0, may hold values from 0 to 999
- frame_times: int32 [32], P('groups'), parts along dimension 0, may hold values from 0 to 30, as said below
Outputs:
- advanced: bfloat16 [4096, 2048], P(('groups', 'frame')), parts along dimension 0
There are 2 independent parts, one for each index of `groups`. A program takes and returns all parts, laid end to end along the dimension named above; an argument that names none is the same for every part. Nothing has to cross between parts.
Inputs may be any that keep to these rules, and one draw needn't show every extreme that they name: Rows of queries may be large multiples of key rows. `frame_times`: strictly increasing along the window, starting at 0; neighbouring frames differ by 1 to 3; the last frame stands at 30.
All inputs are finite; a program needn't handle non-finite values.
Results may differ from a plain program's by a relative error of at most 0.009.
Values may be sent and summed in bfloat16 or wider, within the bound.
No kernel may reach another device: no remote copies, remote signals or barrier semaphores. Data moves between devices by JAX's collectives and lax.ppermute only.
A program may use at most 64 MiB of HBM per device.

v0:
```python
import functools
import math

import jax
import jax.numpy as jnp
from jax import lax
from jax.experimental import pallas as pl
from jax.experimental.pallas import tpu as pltpu
from jax.sharding import PartitionSpec as P


LEVELS = 1000
FAR = 1e30
VMEM_BYTES = 24 << 20
SUBLANES = 8
EARLY = 2
LOG2_E = math.log2(math.e)
VMEM = pl.BlockSpec(memory_space=pltpu.VMEM)
SMEM = pl.BlockSpec(memory_space=pltpu.SMEM)
HBM = pl.BlockSpec(memory_space=pltpu.HBM)
ANY = pl.BlockSpec(memory_space=pl.ANY)


def shifted(value, axis, steps):
    count = lax.axis_size(axis)
    first, last = (max(0, -steps), min(count, count - steps))
    return lax.ppermute(value, axis, [(source, source + steps) for source in range(first, last)])


def paired(value, step):
    count = lax.axis_size("frame")
    return lax.ppermute(value, "frame", [(device, device ^ step) for device in range(count)])


def noise_gates(noise_level):
    phase = (noise_level.astype(jnp.float32) / LEVELS + 0.008) / 1.008
    cosine = jnp.cos(phase * (math.pi / 2))
    signal = cosine * cosine
    return (jnp.sqrt(signal), jnp.sqrt(1.0 - signal))


def in_pairs(frame_rows, count):
    return frame_rows % (SUBLANES * count) == 0 and count >= 4 and count & (count - 1) == 0


def far_steps(count):
    half, quarter = count // 2, count // 4
    return [half + offset + side for offset in range(quarter) for side in (quarter, 0)]


def near_steps(count):
    return list(range(count // 2 - 1, 0, -1))


def attend_heads(query_of, key_of, value_of, slope_of, distance, head_count, head_dim):
    factor = LOG2_E / math.sqrt(head_dim)
    heads = range(head_count)
    scores = [
        lax.dot_general(key_of(head), query_of(head), (((1,), (1,)), ((), ())), preferred_element_type=jnp.float32)
        * factor
        for head in heads
    ]
    if distance is not None:
        scores = [score - (slope_of(head) * LOG2_E) * distance for score, head in zip(scores, heads)]
    peaks = [jnp.max(score, axis=0, keepdims=True) for score in scores]
    raised = [jnp.exp2(score - peak) for score, peak in zip(scores, peaks)]
    shares = [1.0 / jnp.sum(value, axis=0, keepdims=True) for value in raised]
    weights = [(value * share).astype(jnp.bfloat16) for value, share in zip(raised, shares)]
    return [
        lax.dot_general(weight, value_of(head), (((0,), (0,)), ((), ())), preferred_element_type=jnp.float32)
        for weight, head in zip(weights, heads)
    ]


def run_copies(sem, pairs):
    copies = [pltpu.make_async_copy(source, target, sem.at[place]) for place, (source, target) in enumerate(pairs)]
    for copy in copies:
        copy.start()
    for copy in copies:
        copy.wait()


def rows_at(ref, block, share):
    return ref.at[pl.ds(pl.multiple_of(block * share, share), share), :]


def gather_kernel(steps, share, width, query_ref, key_ref, value_ref, *rest):
    outs, sem = rest[:-1], rest[-1]
    me = lax.axis_index("frame")
    pairs = []
    for place, step in enumerate(steps):
        start = pl.multiple_of((me ^ step) * share, share)
        for part, source in enumerate((query_ref, key_ref, value_ref)):
            pairs.append(
                (source.at[pl.ds(start, share), pl.ds(0, width)], outs[place].at[:, pl.ds(part * width, width)])
            )
    run_copies(sem, pairs)


def paired_kernel(count, head_dim, share, slopes_ref, distance_ref, gate_ref, *rest):
    blocks, out_ref, moved_ref, result_ref, sem = rest[:count], *rest[count:]
    width = result_ref.shape[1]
    gate = gate_ref[...]
    for step, block in enumerate(blocks):
        moved_ref[pl.ds(step * share, share), :] = block[...]
    part = lambda index: lambda head: moved_ref[:, pl.ds(index * width + head * head_dim, head_dim)]
    attended = attend_heads(
        part(0), part(1), part(2), lambda head: slopes_ref[head], distance_ref[...], width // head_dim, head_dim
    )
    for head, value in enumerate(attended):
        result_ref[:, pl.ds(head * head_dim, head_dim)] = (value * gate).astype(result_ref.dtype)
    me = lax.axis_index("frame")
    pairs = []
    for step in range(count):
        slot = lax.rem((me ^ step) + count - 1, count)
        pairs.append((result_ref.at[pl.ds(step * share, share), :], rows_at(out_ref, slot, share)))
    run_copies(sem, pairs)


def plain_kernel(head_dim, share, slopes_ref, distance_ref, gate_ref, moved_ref, out_ref):
    rows, width = out_ref.shape
    gate = gate_ref[...]
    kept = lax.broadcasted_iota(jnp.int32, (rows, head_dim), 0) < rows - share
    part = lambda index: lambda head: moved_ref[:, pl.ds(index * width + head * head_dim, head_dim)]
    attended = attend_heads(
        part(0), part(1), part(2), lambda head: slopes_ref[head], distance_ref[...], width // head_dim, head_dim
    )
    for head, value in enumerate(attended):
        earlier = pltpu.roll(value * gate, rows - share, 0)
        out_ref[:, pl.ds(head * head_dim, head_dim)] = jnp.where(kept, earlier, 0.0).astype(out_ref.dtype)


def spatial_kernel(head_dim, gate_ref, query_ref, key_ref, value_ref, out_ref):
    width = out_ref.shape[1]
    gate = gate_ref[lax.axis_index("frame")]
    part = lambda ref: lambda head: ref[:, pl.ds(head * head_dim, head_dim)]
    attended = attend_heads(part(query_ref), part(key_ref), part(value_ref), None, None, width // head_dim, head_dim)
    for head, value in enumerate(attended):
        out_ref[:, pl.ds(head * head_dim, head_dim)] = (value * gate).astype(out_ref.dtype)


def cost(rows, width, operands):
    return pl.CostEstimate(
        flops=4 * rows * rows * width, bytes_accessed=operands * 2 * rows * width, transcendentals=rows * rows * 16
    )


def params():
    return pltpu.CompilerParams(vmem_limit_bytes=VMEM_BYTES)


def table_kernel(crossed, share, times_ref, gate_ref, distance_ref, rows_ref):
    rows, width = distance_ref.shape[0], rows_ref.shape[1]
    count = rows // share
    me = lax.axis_index("frame")
    owners = [me ^ place if crossed else place for place in range(count)]
    times = [times_ref[owner].astype(jnp.float32) for owner in owners]
    lane = lax.broadcasted_iota(jnp.int32, (share, rows), 1)
    row = lax.broadcasted_iota(jnp.int32, (share, rows), 0)
    lane_times = jnp.zeros((share, rows), jnp.float32)
    for place, time in enumerate(times):
        lane_times = jnp.where(lax.div(lane, share) == place, time, lane_times)
    same = lax.rem(lane, share) == row
    for place, (owner, time) in enumerate(zip(owners, times)):
        span = pl.ds(place * share, share)
        distance_ref[span, :] = jnp.where(same, jnp.abs(lane_times - time), FAR)
        gate = jnp.where(owner > 0, gate_ref[owner], 0.0)
        rows_ref[span, :] = jnp.full((share, width), gate, jnp.float32)


def tables(frame_times, noise_gate, crossed, share, head_dim):
    rows = frame_times.shape[0] * share
    return pl.pallas_call(
        functools.partial(table_kernel, crossed, share),
        out_shape=[
            jax.ShapeDtypeStruct((rows, rows), jnp.float32),
            jax.ShapeDtypeStruct((rows, head_dim), jnp.float32),
        ],
        in_specs=[SMEM, SMEM],
        out_specs=[VMEM, VMEM],
        compiler_params=params(),
        name="tables",
    )(frame_times, noise_gate)


def spatial_part(queries, key_rows, value_rows, signal_gate, head_dim):
    frame_rows, model_width = queries.shape
    spatial = pl.pallas_call(
        functools.partial(spatial_kernel, head_dim),
        out_shape=jax.ShapeDtypeStruct((frame_rows, model_width), jnp.bfloat16),
        in_specs=[SMEM, VMEM, VMEM, VMEM],
        out_specs=VMEM,
        cost_estimate=cost(frame_rows, model_width, 4),
        compiler_params=params(),
        name="spatial",
    )(signal_gate, queries, key_rows, value_rows)
    return shifted(spatial, "frame", -1)


def exchanged(arrays, slopes, distance, gate_rows, head_dim, share):
    rows, width = arrays[0].shape
    moved = lax.all_to_all(jnp.concatenate(arrays, axis=1), "frame", split_axis=0, concat_axis=0, tiled=True)
    temporal = pl.pallas_call(
        functools.partial(plain_kernel, head_dim, share),
        out_shape=jax.ShapeDtypeStruct((rows, width), jnp.bfloat16),
        in_specs=[SMEM, VMEM, VMEM, VMEM],
        out_specs=VMEM,
        cost_estimate=cost(rows, width, 4),
        compiler_params=params(),
        name="temporalb",
    )(slopes, distance, gate_rows, moved)
    return lax.all_to_all(temporal, "frame", split_axis=0, concat_axis=0, tiled=True)


def permuted(arrays, slopes, distance, gate_rows, head_dim, share):
    (rows, width), count = arrays[0].shape, lax.axis_size("frame")
    held = [pltpu.with_memory_space_constraint(value, pltpu.HBM) for value in arrays]

    def gathered(some):
        return pl.pallas_call(
            functools.partial(gather_kernel, some, share, width),
            out_shape=[pltpu.VMEM((share, 3 * width), jnp.bfloat16) for _ in some],
            in_specs=[HBM] * 3,
            out_specs=[VMEM] * len(some),
            scratch_shapes=[pltpu.SemaphoreType.DMA((3 * len(some),))],
            compiler_params=params(),
            name="gather",
        )(*held)

    order = far_steps(count) + near_steps(count) + [0]
    blocks = dict(zip(order, [*gathered(order[:EARLY]), *gathered(order[EARLY:])]))
    landed = []
    for step in range(count):
        block = paired(blocks[step], step) if step else blocks[step]
        landed.append(pltpu.with_memory_space_constraint(block, pltpu.VMEM))
    temporal = pl.pallas_call(
        functools.partial(paired_kernel, count, head_dim, share),
        out_shape=jax.ShapeDtypeStruct((rows, width), jnp.bfloat16),
        in_specs=[SMEM, VMEM, VMEM] + [VMEM] * count,
        out_specs=HBM,
        scratch_shapes=[
            pltpu.VMEM((rows, 3 * width), jnp.bfloat16),
            pltpu.VMEM((rows, width), jnp.bfloat16),
            pltpu.SemaphoreType.DMA((count,)),
        ],
        cost_estimate=cost(rows, width, 4),
        compiler_params=params(),
        name="temporal",
    )(slopes, distance, gate_rows, *landed)
    return lax.all_to_all(temporal, "frame", split_axis=0, concat_axis=0, tiled=True)


def body(queries, key_rows, value_rows, slopes, noise_level, frame_times):
    frame_rows, model_width = queries.shape
    head_count = slopes.shape[0]
    head_dim = model_width // head_count
    count = lax.axis_size("frame")
    share = frame_rows // count
    signal_gate, noise_gate = noise_gates(noise_level)
    slopes = slopes.astype(jnp.float32)
    arrays = (queries, key_rows, value_rows)
    carried = spatial_part(*arrays, signal_gate, head_dim)
    paired_up = in_pairs(frame_rows, count)
    distance, gate_rows = tables(frame_times, noise_gate, paired_up, share, head_dim)
    spread = permuted if paired_up else exchanged
    temporal = spread(arrays, slopes, distance, gate_rows, head_dim, share)
    return (carried.astype(jnp.float32) + temporal.astype(jnp.float32)).astype(jnp.bfloat16)


def solution(mesh):
    return jax.shard_map(
        body,
        mesh=mesh,
        in_specs=(
            P(("groups", "frame"), None),
            P(("groups", "frame"), None),
            P(("groups", "frame"), None),
            P(),
            P("groups"),
            P("groups"),
        ),
        out_specs=P(("groups", "frame"), None),
        check_vma=False,
    )
```

profile of v0, /device:TPU:13, one launch (start us, length us, event | category | flops | bytes accessed | tf_op | source)
XLA Modules:
  0.0 75.1 jit_solution(8111313528263160810)
XLA Ops:
  0.0 1.6 %gather.2 = (bf16[8,6144]{1,0:T(8,128)(2,1)S(1)}, bf16[8,6144]{1,0:T(8,128)(2,1)S(1)}, bf16[8,6144]{1,0:T(8,128)(2,1)S(1)}, bf16[8,6144]{1,0:T(8,128)(2,1)S(1)},...) custom-call(bf16[128,2048]{1,0:T(8,128)(2,1)} %query_ref.5, ...), custom_call_target="tpu_custom_call" | custom-call | tf_op jit(solution)/shard_map/gather/pallas_call | solution.py:220
  1.6 0.7 collective-permute-start.1
  2.4 2.3 %collective-permute-start.10 = (bf16[8,6144]{1,0:T(8,128)(2,1)S(1)}, bf16[8,6144]{1,0:T(8,128)(2,1)S(1)}, u32[]{:S(2)}, u32[]{:S(2)}) collective-permute-start(bf16[8,6144]{1,0:T(8,128)(2,1)S(1)} %get-tuple-element.35), channel_id=1, source_target_pairs={{0,10},{1,11},{2,8},{3,9},{4,14},{5,15},{6,12},{7,13},{8,2},{9,3},... | collective-permute-start | bytes 294920 | tf_op jit(solution)/shard_map/ppermute | solution.py:32
  4.6 1.3 %collective-permute-start.11 = (bf16[8,6144]{1,0:T(8,128)(2,1)S(1)}, bf16[8,6144]{1,0:T(8,128)(2,1)S(1)}, u32[]{:S(2)}, u32[]{:S(2)}) collective-permute-start(bf16[8,6144]{1,0:T(8,128)(2,1)S(1)} %get-tuple-element.36), channel_id=1, source_target_pairs={{0,11},{1,10},{2,9},{3,8},{4,15},{5,14},{6,13},{7,12},{8,3},{9,2},... | collective-permute-start | bytes 294920 | tf_op jit(solution)/shard_map/ppermute | solution.py:32
  5.9 1.3 %collective-permute-start.13 = (bf16[8,6144]{1,0:T(8,128)(2,1)S(1)}, bf16[8,6144]{1,0:T(8,128)(2,1)S(1)}, u32[]{:S(2)}, u32[]{:S(2)}) collective-permute-start(bf16[8,6144]{1,0:T(8,128)(2,1)S(1)} %get-tuple-element.38), channel_id=1, source_target_pairs={{0,13},{1,12},{2,15},{3,14},{4,9},{5,8},{6,11},{7,10},{8,5},{9,4},... | collective-permute-start | bytes 294920 | tf_op jit(solution)/shard_map/ppermute | solution.py:32
  7.2 0.1 collective-permute-start.14
  7.3 2.8 %collective-permute-start.15 = (bf16[8,6144]{1,0:T(8,128)(2,1)S(1)}, bf16[8,6144]{1,0:T(8,128)(2,1)S(1)}, u32[]{:S(2)}, u32[]{:S(2)}) collective-permute-start(bf16[8,6144]{1,0:T(8,128)(2,1)S(1)} %get-tuple-element.40), channel_id=1, source_target_pairs={{0,15},{1,14},{2,13},{3,12},{4,11},{5,10},{6,9},{7,8},{8,7},{9,6},... | collective-permute-start | bytes 294920 | tf_op jit(solution)/shard_map/ppermute | solution.py:32
  10.1 7.5 %collective-permute-done.10.rest_10_ = bf16[8,6144]{1,0:T(8,128)(2,1)S(1)} collective-permute-done((bf16[8,6144]{1,0:T(8,128)(2,1)S(1)}, bf16[8,6144]{1,0:T(8,128)(2,1)S(1)}, u32[]{:S(2)}, u32[]{:S(2)}) %collective-permute-start.10) | collective-permute-done | bytes 98336 | tf_op jit(solution)/shard_map/ppermute | solution.py:32
  17.6 1.2 %collective-permute-start.2 = (bf16[8,6144]{1,0:T(8,128)(2,1)S(1)}, bf16[8,6144]{1,0:T(8,128)(2,1)S(1)}, u32[]{:S(2)}, u32[]{:S(2)}) collective-permute-start(bf16[8,6144]{1,0:T(8,128)(2,1)S(1)} %get-tuple-element.27), channel_id=1, source_target_pairs={{0,2},{1,3},{2,0},{3,1},{4,6},{5,7},{6,4},{7,5},{8,10},{9,11},{10,... | collective-permute-start | bytes 294920 | tf_op jit(solution)/shard_map/ppermute | solution.py:32
  18.9 0.9 %collective-permute-done.11.rest_11_ = bf16[8,6144]{1,0:T(8,128)(2,1)S(1)} collective-permute-done((bf16[8,6144]{1,0:T(8,128)(2,1)S(1)}, bf16[8,6144]{1,0:T(8,128)(2,1)S(1)}, u32[]{:S(2)}, u32[]{:S(2)}) %collective-permute-start.11) | collective-permute-done | bytes 98336 | tf_op jit(solution)/shard_map/ppermute | solution.py:32
  19.7 1.6 %collective-permute-start.3 = (bf16[8,6144]{1,0:T(8,128)(2,1)S(1)}, bf16[8,6144]{1,0:T(8,128)(2,1)S(1)}, u32[]{:S(2)}, u32[]{:S(2)}) collective-permute-start(bf16[8,6144]{1,0:T(8,128)(2,1)S(1)} %get-tuple-element.28), channel_id=1, source_target_pairs={{0,3},{1,2},{2,1},{3,0},{4,7},{5,6},{6,5},{7,4},{8,11},{9,10},{10,... | collective-permute-start | bytes 294920 | tf_op jit(solution)/shard_map/ppermute | solution.py:32
  21.3 0.7 collective-permute-done.13.rest_13_
  22.0 0.2 collective-permute-start.4
  22.3 2.1 %collective-permute-done.14.rest_14_ = bf16[8,6144]{1,0:T(8,128)(2,1)S(1)} collective-permute-done((bf16[8,6144]{1,0:T(8,128)(2,1)S(1)}, bf16[8,6144]{1,0:T(8,128)(2,1)S(1)}, u32[]{:S(2)}, u32[]{:S(2)}) %collective-permute-start.14) | collective-permute-done | bytes 98336 | tf_op jit(solution)/shard_map/ppermute | solution.py:32
  24.3 0.9 %gather.3 = (bf16[8,6144]{1,0:T(8,128)(2,1)S(1)}, bf16[8,6144]{1,0:T(8,128)(2,1)S(1)}) custom-call(bf16[128,2048]{1,0:T(8,128)(2,1)} %query_ref.5, bf16[128,2048]{1,0:T(8,128)(2,1)} %key_ref.5, bf16[128,2048]{1,0:T(8,128)(2,1)} %value_ref.5), custom_call_target="tpu_custom_call" | custom-call | tf_op jit(solution)/shard_map/gather/pallas_call | solution.py:220
  25.2 1.5 %collective-permute-done.15.rest_15_ = bf16[8,6144]{1,0:T(8,128)(2,1)S(1)} collective-permute-done((bf16[8,6144]{1,0:T(8,128)(2,1)S(1)}, bf16[8,6144]{1,0:T(8,128)(2,1)S(1)}, u32[]{:S(2)}, u32[]{:S(2)}) %collective-permute-start.15) | collective-permute-done | bytes 98336 | tf_op jit(solution)/shard_map/ppermute | solution.py:32
  26.7 1.1 %collective-permute-start.6 = (bf16[8,6144]{1,0:T(8,128)(2,1)S(1)}, bf16[8,6144]{1,0:T(8,128)(2,1)S(1)}, u32[]{:S(2)}, u32[]{:S(2)}) collective-permute-start(bf16[8,6144]{1,0:T(8,128)(2,1)S(1)} %get-tuple-element.31), channel_id=1, source_target_pairs={{0,6},{1,7},{2,4},{3,5},{4,2},{5,3},{6,0},{7,1},{8,14},{9,15},{10,... | collective-permute-start | bytes 294920 | tf_op jit(solution)/shard_map/ppermute | solution.py:32
  27.9 1.6 %collective-permute-start.7 = (bf16[8,6144]{1,0:T(8,128)(2,1)S(1)}, bf16[8,6144]{1,0:T(8,128)(2,1)S(1)}, u32[]{:S(2)}, u32[]{:S(2)}) collective-permute-start(bf16[8,6144]{1,0:T(8,128)(2,1)S(1)} %get-tuple-element.32), channel_id=1, source_target_pairs={{0,7},{1,6},{2,5},{3,4},{4,3},{5,2},{6,1},{7,0},{8,15},{9,14},{10,... | collective-permute-start | bytes 294920 | tf_op jit(solution)/shard_map/ppermute | solution.py:32
  29.4 2.8 %collective-permute-start.9 = (bf16[8,6144]{1,0:T(8,128)(2,1)S(1)}, bf16[8,6144]{1,0:T(8,128)(2,1)S(1)}, u32[]{:S(2)}, u32[]{:S(2)}) collective-permute-start(bf16[8,6144]{1,0:T(8,128)(2,1)S(1)} %get-tuple-element.34), channel_id=1, source_target_pairs={{0,9},{1,8},{2,11},{3,10},{4,13},{5,12},{6,15},{7,14},{8,1},{9,0},... | collective-permute-start | bytes 294920 | tf_op jit(solution)/shard_map/ppermute | solution.py:32
  32.3 2.8 %collective-permute-start.8 = (bf16[8,6144]{1,0:T(8,128)(2,1)S(1)}, bf16[8,6144]{1,0:T(8,128)(2,1)S(1)}, u32[]{:S(2)}, u32[]{:S(2)}) collective-permute-start(bf16[8,6144]{1,0:T(8,128)(2,1)S(1)} %get-tuple-element.33), channel_id=1, source_target_pairs={{0,8},{1,9},{2,10},{3,11},{4,12},{5,13},{6,14},{7,15},{8,0},{9,1},... | collective-permute-start | bytes 294920 | tf_op jit(solution)/shard_map/ppermute | solution.py:32
  35.1 0.1 subtract_sqrt_fusion
  35.2 0.6 copy-done.3
  35.9 0.6 tables.1
  36.5 4.3 %collective-permute-done.9.rest_9_ = bf16[8,6144]{1,0:T(8,128)(2,1)S(1)} collective-permute-done((bf16[8,6144]{1,0:T(8,128)(2,1)S(1)}, bf16[8,6144]{1,0:T(8,128)(2,1)S(1)}, u32[]{:S(2)}, u32[]{:S(2)}) %collective-permute-start.9) | collective-permute-done | bytes 98336 | tf_op jit(solution)/shard_map/ppermute | solution.py:32
  40.7 3.0 %collective-permute-done.12.rest_12_ = bf16[8,6144]{1,0:T(8,128)(2,1)S(1)} collective-permute-done((bf16[8,6144]{1,0:T(8,128)(2,1)S(1)}, bf16[8,6144]{1,0:T(8,128)(2,1)S(1)}, u32[]{:S(2)}, u32[]{:S(2)}) %collective-permute-start.12) | collective-permute-done | bytes 98336 | tf_op jit(solution)/shard_map/ppermute | solution.py:32
  43.8 1.2 %collective-permute-done.8.rest_8_ = bf16[8,6144]{1,0:T(8,128)(2,1)S(1)} collective-permute-done((bf16[8,6144]{1,0:T(8,128)(2,1)S(1)}, bf16[8,6144]{1,0:T(8,128)(2,1)S(1)}, u32[]{:S(2)}, u32[]{:S(2)}) %collective-permute-start.8) | collective-permute-done | bytes 98336 | tf_op jit(solution)/shard_map/ppermute | solution.py:32
  45.0 2.4 %temporal.1 = bf16[128,2048]{1,0:T(8,128)(2,1)} custom-call(f32[16]{0:T(128)S(1)} %convert_element_type.20.slopes_ref, f32[128,128]{1,0:T(8,128)S(1)} %get-tuple-element.23.distance_ref, f32[128,128]{1,0:T(8,128)S(1)} %get-tuple-element.24.gate_ref, bf16[8,6144]{1,0:T(8,128)(2,1)S(1)} %get-tuple-element.25.rest_0_, ...), custom_call_target="tpu_custom_call" | custom-call | flops 134217728 | bytes 2097152 | tf_op jit(solution)/shard_map/temporal/pallas_call | solution.py:236
  47.4 7.6 %all-to-all-start = ((bf16[16,8,2048]{2,1,0:T(8,128)(2,1)}), bf16[16,8,2048]{2,1,0:T(8,128)(2,1)S(1)}, u32[]{:S(2)}, u32[]{:S(2)}) async-start(bf16[16,8,2048]{2,1,0:T(8,128)(2,1)} %bitcast), calls=%async_computation | async-start | bytes 1048576 | tf_op jit(solution)/shard_map/all_to_all | solution.py:250
  55.0 1.4 %spatial.1 = bf16[128,2048]{1,0:T(8,128)(2,1)S(1)} custom-call(f32[16]{0:T(128)S(1)} %get-tuple-element.42.gate_ref, bf16[128,2048]{1,0:T(8,128)(2,1)S(1)} %copy-done, bf16[128,2048]{1,0:T(8,128)(2,1)S(1)} %copy-done.1, bf16[128,2048]{1,0:T(8,128)(2,1)S(1)} %copy-done.2), custom_call_target="tpu_custom_call" | custom-call | flops 134217728 | bytes 2097152 | tf_op jit(solution)/shard_map/spatial/pallas_call | solution.py:188
  56.4 2.3 %collective-permute-start = (bf16[128,2048]{1,0:T(8,128)(2,1)S(1)}, bf16[128,2048]{1,0:T(8,128)(2,1)S(1)}, u32[]{:S(2)}, u32[]{:S(2)}) collective-permute-start(bf16[128,2048]{1,0:T(8,128)(2,1)S(1)} %spatial.1), channel_id=1, source_target_pairs={{1,0},{2,1},{3,2},{4,3},{5,4},{6,5},{7,6},{8,7},{9,8},{10,9},{11,1... | collective-permute-start | bytes 1572872 | tf_op jit(solution)/shard_map/ppermute | solution.py:27
  58.7 15.5 %collective-permute-done = bf16[128,2048]{1,0:T(8,128)(2,1)S(1)} collective-permute-done((bf16[128,2048]{1,0:T(8,128)(2,1)S(1)}, bf16[128,2048]{1,0:T(8,128)(2,1)S(1)}, u32[]{:S(2)}, u32[]{:S(2)}) %collective-permute-start) | collective-permute-done | bytes 524320 | tf_op jit(solution)/shard_map/ppermute | solution.py:27
  74.2 0.9 %fusion = bf16[128,2048]{1,0:T(8,128)(2,1)} fusion(bf16[128,2048]{1,0:T(8,128)(2,1)S(1)} %collective-permute-done, bf16[16,8,2048]{2,1,0:T(8,128)(2,1)S(1)} %all-to-all-done), kind=kLoop, calls=%fused_computation.1 | loop fusion | flops 1048576 | bytes 1572864 | tf_op jit(solution)/shard_map/convert_element_type | solution.py:267
  (22 shorter events, 0.1 us)
Async XLA Ops:
  1.6 5.7 %collective-permute-start.1 = (bf16[8,6144]{1,0:T(8,128)(2,1)S(1)}, bf16[8,6144]{1,0:T(8,128)(2,1)S(1)}, u32[]{:S(2)}, u32[]{:S(2)}) collective-permute-start(bf16[8,6144]{1,0:T(8,128)(2,1)S(1)} %get-tuple-element.26), channel_id=1, source_target_pairs={{0,1},{1,0},{2,3},{3,2},{4,5},{5,4},{6,7},{7,6},{8,9},{9,8},{10,11... | collective-permute-start | bytes 294920 | tf_op jit(solution)/shard_map/ppermute | solution.py:32
  2.4 15.2 %collective-permute-start.10 = (bf16[8,6144]{1,0:T(8,128)(2,1)S(1)}, bf16[8,6144]{1,0:T(8,128)(2,1)S(1)}, u32[]{:S(2)}, u32[]{:S(2)}) collective-permute-start(bf16[8,6144]{1,0:T(8,128)(2,1)S(1)} %get-tuple-element.35), channel_id=1, source_target_pairs={{0,10},{1,11},{2,8},{3,9},{4,14},{5,15},{6,12},{7,13},{8,2},{9,3},... | collective-permute-start | bytes 294920 | tf_op jit(solution)/shard_map/ppermute | solution.py:32
  4.6 15.1 %collective-permute-start.11 = (bf16[8,6144]{1,0:T(8,128)(2,1)S(1)}, bf16[8,6144]{1,0:T(8,128)(2,1)S(1)}, u32[]{:S(2)}, u32[]{:S(2)}) collective-permute-start(bf16[8,6144]{1,0:T(8,128)(2,1)S(1)} %get-tuple-element.36), channel_id=1, source_target_pairs={{0,11},{1,10},{2,9},{3,8},{4,15},{5,14},{6,13},{7,12},{8,3},{9,2},... | collective-permute-start | bytes 294920 | tf_op jit(solution)/shard_map/ppermute | solution.py:32
  5.9 16.1 %collective-permute-start.13 = (bf16[8,6144]{1,0:T(8,128)(2,1)S(1)}, bf16[8,6144]{1,0:T(8,128)(2,1)S(1)}, u32[]{:S(2)}, u32[]{:S(2)}) collective-permute-start(bf16[8,6144]{1,0:T(8,128)(2,1)S(1)} %get-tuple-element.38), channel_id=1, source_target_pairs={{0,13},{1,12},{2,15},{3,14},{4,9},{5,8},{6,11},{7,10},{8,5},{9,4},... | collective-permute-start | bytes 294920 | tf_op jit(solution)/shard_map/ppermute | solution.py:32
  7.2 17.1 %collective-permute-start.14 = (bf16[8,6144]{1,0:T(8,128)(2,1)S(1)}, bf16[8,6144]{1,0:T(8,128)(2,1)S(1)}, u32[]{:S(2)}, u32[]{:S(2)}) collective-permute-start(bf16[8,6144]{1,0:T(8,128)(2,1)S(1)} %get-tuple-element.39), channel_id=1, source_target_pairs={{0,14},{1,15},{2,12},{3,13},{4,10},{5,11},{6,8},{7,9},{8,6},{9,7},... | collective-permute-start | bytes 294920 | tf_op jit(solution)/shard_map/ppermute | solution.py:32
  7.3 19.4 %collective-permute-start.15 = (bf16[8,6144]{1,0:T(8,128)(2,1)S(1)}, bf16[8,6144]{1,0:T(8,128)(2,1)S(1)}, u32[]{:S(2)}, u32[]{:S(2)}) collective-permute-start(bf16[8,6144]{1,0:T(8,128)(2,1)S(1)} %get-tuple-element.40), channel_id=1, source_target_pairs={{0,15},{1,14},{2,13},{3,12},{4,11},{5,10},{6,9},{7,8},{8,7},{9,6},... | collective-permute-start | bytes 294920 | tf_op jit(solution)/shard_map/ppermute | solution.py:32
  17.6 10.2 %collective-permute-start.2 = (bf16[8,6144]{1,0:T(8,128)(2,1)S(1)}, bf16[8,6144]{1,0:T(8,128)(2,1)S(1)}, u32[]{:S(2)}, u32[]{:S(2)}) collective-permute-start(bf16[8,6144]{1,0:T(8,128)(2,1)S(1)} %get-tuple-element.27), channel_id=1, source_target_pairs={{0,2},{1,3},{2,0},{3,1},{4,6},{5,7},{6,4},{7,5},{8,10},{9,11},{10,... | collective-permute-start | bytes 294920 | tf_op jit(solution)/shard_map/ppermute | solution.py:32
  19.7 9.7 %collective-permute-start.3 = (bf16[8,6144]{1,0:T(8,128)(2,1)S(1)}, bf16[8,6144]{1,0:T(8,128)(2,1)S(1)}, u32[]{:S(2)}, u32[]{:S(2)}) collective-permute-start(bf16[8,6144]{1,0:T(8,128)(2,1)S(1)} %get-tuple-element.28), channel_id=1, source_target_pairs={{0,3},{1,2},{2,1},{3,0},{4,7},{5,6},{6,5},{7,4},{8,11},{9,10},{10,... | collective-permute-start | bytes 294920 | tf_op jit(solution)/shard_map/ppermute | solution.py:32
  22.0 10.2 %collective-permute-start.4 = (bf16[8,6144]{1,0:T(8,128)(2,1)S(1)}, bf16[8,6144]{1,0:T(8,128)(2,1)S(1)}, u32[]{:S(2)}, u32[]{:S(2)}) collective-permute-start(bf16[8,6144]{1,0:T(8,128)(2,1)S(1)} %get-tuple-element.29), channel_id=1, source_target_pairs={{0,4},{1,5},{2,6},{3,7},{4,0},{5,1},{6,2},{7,3},{8,12},{9,13},{10,... | collective-permute-start | bytes 294920 | tf_op jit(solution)/shard_map/ppermute | solution.py:32
  24.3 8.0 %collective-permute-start.5 = (bf16[8,6144]{1,0:T(8,128)(2,1)S(1)}, bf16[8,6144]{1,0:T(8,128)(2,1)S(1)}, u32[]{:S(2)}, u32[]{:S(2)}) collective-permute-start(bf16[8,6144]{1,0:T(8,128)(2,1)S(1)} %get-tuple-element.30), channel_id=1, source_target_pairs={{0,5},{1,4},{2,7},{3,6},{4,1},{5,0},{6,3},{7,2},{8,13},{9,12},{10,... | collective-permute-start | bytes 294920 | tf_op jit(solution)/shard_map/ppermute | solution.py:32
  26.7 9.7 %collective-permute-start.6 = (bf16[8,6144]{1,0:T(8,128)(2,1)S(1)}, bf16[8,6144]{1,0:T(8,128)(2,1)S(1)}, u32[]{:S(2)}, u32[]{:S(2)}) collective-permute-start(bf16[8,6144]{1,0:T(8,128)(2,1)S(1)} %get-tuple-element.31), channel_id=1, source_target_pairs={{0,6},{1,7},{2,4},{3,5},{4,2},{5,3},{6,0},{7,1},{8,14},{9,15},{10,... | collective-permute-start | bytes 294920 | tf_op jit(solution)/shard_map/ppermute | solution.py:32
  27.9 8.6 %collective-permute-start.7 = (bf16[8,6144]{1,0:T(8,128)(2,1)S(1)}, bf16[8,6144]{1,0:T(8,128)(2,1)S(1)}, u32[]{:S(2)}, u32[]{:S(2)}) collective-permute-start(bf16[8,6144]{1,0:T(8,128)(2,1)S(1)} %get-tuple-element.32), channel_id=1, source_target_pairs={{0,7},{1,6},{2,5},{3,4},{4,3},{5,2},{6,1},{7,0},{8,15},{9,14},{10,... | collective-permute-start | bytes 294920 | tf_op jit(solution)/shard_map/ppermute | solution.py:32
  29.4 11.3 %collective-permute-start.9 = (bf16[8,6144]{1,0:T(8,128)(2,1)S(1)}, bf16[8,6144]{1,0:T(8,128)(2,1)S(1)}, u32[]{:S(2)}, u32[]{:S(2)}) collective-permute-start(bf16[8,6144]{1,0:T(8,128)(2,1)S(1)} %get-tuple-element.34), channel_id=1, source_target_pairs={{0,9},{1,8},{2,11},{3,10},{4,13},{5,12},{6,15},{7,14},{8,1},{9,0},... | collective-permute-start | bytes 294920 | tf_op jit(solution)/shard_map/ppermute | solution.py:32
  32.3 2.9 %copy-start.4 = (s32[16]{0:T(128)S(1)}, s32[16]{0:T(128)}, u32[]{:S(2)}) copy-start(s32[16]{0:T(128)} %param.10) | copy-start | bytes 196
  32.3 11.5 %collective-permute-start.12 = (bf16[8,6144]{1,0:T(8,128)(2,1)S(1)}, bf16[8,6144]{1,0:T(8,128)(2,1)S(1)}, u32[]{:S(2)}, u32[]{:S(2)}) collective-permute-start(bf16[8,6144]{1,0:T(8,128)(2,1)S(1)} %get-tuple-element.37), channel_id=1, source_target_pairs={{0,12},{1,13},{2,14},{3,15},{4,8},{5,9},{6,10},{7,11},{8,4},{9,5},... | collective-permute-start | bytes 294920 | tf_op jit(solution)/shard_map/ppermute | solution.py:32
  32.3 2.9 %copy-start.5 = (bf16[16]{0:T(256)(128)(2,1)S(1)}, bf16[16]{0:T(256)(128)(2,1)}, u32[]{:S(2)}) copy-start(bf16[16]{0:T(256)(128)(2,1)} %param.9) | copy-start | bytes 100
  32.3 12.6 %collective-permute-start.8 = (bf16[8,6144]{1,0:T(8,128)(2,1)S(1)}, bf16[8,6144]{1,0:T(8,128)(2,1)S(1)}, u32[]{:S(2)}, u32[]{:S(2)}) collective-permute-start(bf16[8,6144]{1,0:T(8,128)(2,1)S(1)} %get-tuple-element.33), channel_id=1, source_target_pairs={{0,8},{1,9},{2,10},{3,11},{4,12},{5,13},{6,14},{7,15},{8,0},{9,1},... | collective-permute-start | bytes 294920 | tf_op jit(solution)/shard_map/ppermute | solution.py:32
  35.2 0.7 copy-start.3
  44.9 10.1 %copy-start.2 = (bf16[128,2048]{1,0:T(8,128)(2,1)S(1)}, bf16[128,2048]{1,0:T(8,128)(2,1)}, u32[]{:S(2)}) copy-start(bf16[128,2048]{1,0:T(8,128)(2,1)} %value_ref.5) | copy-start | bytes 1572868
  47.4 7.7 %copy-start = (bf16[128,2048]{1,0:T(8,128)(2,1)S(1)}, bf16[128,2048]{1,0:T(8,128)(2,1)}, u32[]{:S(2)}) copy-start(bf16[128,2048]{1,0:T(8,128)(2,1)} %query_ref.5) | copy-start | bytes 1572868
  47.4 7.7 %copy-start.1 = (bf16[128,2048]{1,0:T(8,128)(2,1)S(1)}, bf16[128,2048]{1,0:T(8,128)(2,1)}, u32[]{:S(2)}) copy-start(bf16[128,2048]{1,0:T(8,128)(2,1)} %key_ref.5) | copy-start | bytes 1572868
  47.4 26.8 %all-to-all-start = ((bf16[16,8,2048]{2,1,0:T(8,128)(2,1)}), bf16[16,8,2048]{2,1,0:T(8,128)(2,1)S(1)}, u32[]{:S(2)}, u32[]{:S(2)}) async-start(bf16[16,8,2048]{2,1,0:T(8,128)(2,1)} %bitcast), calls=%async_computation | async-start | bytes 1048576 | tf_op jit(solution)/shard_map/all_to_all | solution.py:250
  56.4 17.8 %collective-permute-start = (bf16[128,2048]{1,0:T(8,128)(2,1)S(1)}, bf16[128,2048]{1,0:T(8,128)(2,1)S(1)}, u32[]{:S(2)}, u32[]{:S(2)}) collective-permute-start(bf16[128,2048]{1,0:T(8,128)(2,1)S(1)} %spatial.1), channel_id=1, source_target_pairs={{1,0},{2,1},{3,2},{4,3},{5,4},{6,5},{7,6},{8,7},{9,8},{10,9},{11,1... | collective-permute-start | bytes 1572872 | tf_op jit(solution)/shard_map/ppermute | solution.py:27
where the time goes:
time: 75.6 us; the launch traced here: 75.1 us
  waiting for transfers between devices  36.6 us (48%)
  starting transfers between devices  29.9 us (40%)
  Pallas kernels  6.86 us (9%)
  other arithmetic  0.98 us (1%)
    ppermute x15, waiting for transfers between devices, paired(): lax.ppermute(value, 'frame', [(device, device ^ step) for device in range...  21.1 us
    ppermute x15, starting transfers between devices, paired(): lax.ppermute(value, 'frame', [(device, device ^ step) for device in range...  19.9 us
    ppermute x1, waiting for transfers between devices, shifted(): lax.ppermute(value, axis, [(source, source + steps) for source in range(f...  15.5 us
    all_to_all x1, starting transfers between devices, permuted(): lax.all_to_all(temporal, 'frame', split_axis=0, concat_axis=0, tiled=True)  7.65 us
    pallas_call x2, Pallas kernels, gathered(): pl.pallas_call(functools.partial(gather_kernel, some, share, width), out_...  2.52 us
    pallas_call x1, Pallas kernels, permuted(): pl.pallas_call(functools.partial(paired_kernel, count, head_dim, share),...  2.39 us
    ppermute x1, starting transfers between devices, shifted(): lax.ppermute(value, axis, [(source, source + steps) for source in range(f...  2.31 us
  transfers between devices with their start and end apart: 17, of which 9 were waited for; matrix products, arithmetic and copies ran while one was open for 0% of the time, Pallas kernels for 4%

commit v1 on v0

--- a/solution.py
+++ b/solution.py
@@ -14,6 +14,7 @@
 VMEM_BYTES = 24 << 20
 SUBLANES = 8
 EARLY = 2
+SPLIT = (9, 16)
 LOG2_E = math.log2(math.e)
 VMEM = pl.BlockSpec(memory_space=pltpu.VMEM)
 SMEM = pl.BlockSpec(memory_space=pltpu.SMEM)
@@ -84,36 +85,48 @@
     return ref.at[pl.ds(pl.multiple_of(block * share, share), share), :]
 
 
-def gather_kernel(steps, share, width, query_ref, key_ref, value_ref, *rest):
+def gather_kernel(turns, share, width, query_ref, key_ref, value_ref, *rest):
     outs, sem = rest[:-1], rest[-1]
-    me = lax.axis_index("frame")
-    pairs = []
-    for place, step in enumerate(steps):
-        start = pl.multiple_of((me ^ step) * share, share)
+    chip = lax.axis_index("frame") >> 1
+    rows, pairs = 2 * share, []
+    for place, turn in enumerate(turns):
+        start = pl.multiple_of((chip ^ turn) * rows, rows)
         for part, source in enumerate((query_ref, key_ref, value_ref)):
             pairs.append(
-                (source.at[pl.ds(start, share), pl.ds(0, width)], outs[place].at[:, pl.ds(part * width, width)])
+                (source.at[pl.ds(start, rows), pl.ds(0, width)], outs[place].at[:, pl.ds(part * width, width)])
             )
     run_copies(sem, pairs)
 
 
-def paired_kernel(count, head_dim, share, slopes_ref, distance_ref, gate_ref, *rest):
-    blocks, out_ref, moved_ref, result_ref, sem = rest[:count], *rest[count:]
-    width = result_ref.shape[1]
+def assembly(blocks, sibling_ref, out_ref, share):
+    me = lax.axis_index("frame")
+    core, chip = me & 1, me >> 1
+    pairs = []
+    for turn, block in enumerate(blocks):
+        home = 2 * (chip ^ turn)
+        pairs.append((rows_at(block, core, share), rows_at(out_ref, home + core, share)))
+        pairs.append((sibling_ref.at[pl.ds(turn * share, share), :], rows_at(out_ref, home + 1 - core, share)))
+    return pairs
+
+
+def paired_kernel(turns, head_dim, share, slopes_ref, distance_ref, gate_ref, *rest):
+    blocks, sibling_ref, outs = rest[:turns], rest[turns], rest[turns + 1 : 2 * turns + 1]
+    moved_ref, result_ref, sem = rest[2 * turns + 1 :]
+    run_copies(sem, assembly(blocks, sibling_ref, moved_ref, share))
+    width, count = result_ref.shape[1], 2 * turns
     gate = gate_ref[...]
-    for step, block in enumerate(blocks):
-        moved_ref[pl.ds(step * share, share), :] = block[...]
     part = lambda index: lambda head: moved_ref[:, pl.ds(index * width + head * head_dim, head_dim)]
     attended = attend_heads(
         part(0), part(1), part(2), lambda head: slopes_ref[head], distance_ref[...], width // head_dim, head_dim
     )
     for head, value in enumerate(attended):
         result_ref[:, pl.ds(head * head_dim, head_dim)] = (value * gate).astype(result_ref.dtype)
-    me = lax.axis_index("frame")
+    chip = lax.axis_index("frame") >> 1
     pairs = []
-    for step in range(count):
-        slot = lax.rem((me ^ step) + count - 1, count)
-        pairs.append((result_ref.at[pl.ds(step * share, share), :], rows_at(out_ref, slot, share)))
+    for turn in range(turns):
+        for side in range(2):
+            frame = lax.rem(2 * (chip ^ turn) + side + 1, count)
+            pairs.append((rows_at(result_ref, frame, share), outs[turn].at[pl.ds(side * share, share), :]))
     run_copies(sem, pairs)
 
 
@@ -139,6 +152,18 @@
         out_ref[:, pl.ds(head * head_dim, head_dim)] = (value * gate).astype(out_ref.dtype)
 
 
+def sibling_kernel(share, *refs):
+    blocks, out_ref, sem = refs[:-2], refs[-2], refs[-1]
+    other = 1 - (lax.axis_index("frame") & 1)
+    run_copies(
+        sem, [(rows_at(block, other, share), out_ref.at[pl.ds(turn * share, share), :]) for turn, block in enumerate(blocks)]
+    )
+
+
+def assemble_kernel(share, *refs):
+    run_copies(refs[-1], assembly(refs[:-3], refs[-3], refs[-2], share))
+
+
 def cost(rows, width, operands):
     return pl.CostEstimate(
         flops=4 * rows * rows * width, bytes_accessed=operands * 2 * rows * width, transcendentals=rows * rows * 16
@@ -149,29 +174,27 @@
     return pltpu.CompilerParams(vmem_limit_bytes=VMEM_BYTES)
 
 
-def table_kernel(crossed, share, times_ref, gate_ref, distance_ref, rows_ref):
+def table_kernel(share, times_ref, gate_ref, distance_ref, rows_ref):
     rows, width = distance_ref.shape[0], rows_ref.shape[1]
     count = rows // share
-    me = lax.axis_index("frame")
-    owners = [me ^ place if crossed else place for place in range(count)]
-    times = [times_ref[owner].astype(jnp.float32) for owner in owners]
+    times = [times_ref[place].astype(jnp.float32) for place in range(count)]
     lane = lax.broadcasted_iota(jnp.int32, (share, rows), 1)
     row = lax.broadcasted_iota(jnp.int32, (share, rows), 0)
     lane_times = jnp.zeros((share, rows), jnp.float32)
     for place, time in enumerate(times):
         lane_times = jnp.where(lax.div(lane, share) == place, time, lane_times)
     same = lax.rem(lane, share) == row
-    for place, (owner, time) in enumerate(zip(owners, times)):
+    for place, time in enumerate(times):
         span = pl.ds(place * share, share)
         distance_ref[span, :] = jnp.where(same, jnp.abs(lane_times - time), FAR)
-        gate = jnp.where(owner > 0, gate_ref[owner], 0.0)
+        gate = gate_ref[place] if place else 0.0
         rows_ref[span, :] = jnp.full((share, width), gate, jnp.float32)
 
 
-def tables(frame_times, noise_gate, crossed, share, head_dim):
+def tables(frame_times, noise_gate, share, head_dim):
     rows = frame_times.shape[0] * share
     return pl.pallas_call(
-        functools.partial(table_kernel, crossed, share),
+        functools.partial(table_kernel, share),
         out_shape=[
             jax.ShapeDtypeStruct((rows, rows), jnp.float32),
             jax.ShapeDtypeStruct((rows, head_dim), jnp.float32),
@@ -212,14 +235,35 @@
     return lax.all_to_all(temporal, "frame", split_axis=0, concat_axis=0, tiled=True)
 
 
+def turn_order(count):
+    return [step // 2 for step in far_steps(count) + near_steps(count) if step % 2 == 0]
+
+
+def across_chips(blocks, share):
+    landed = []
+    for turn, block in enumerate(blocks):
+        landed.append(paired(block, 2 * turn) if turn else block)
+    sibling = pl.pallas_call(
+        functools.partial(sibling_kernel, share),
+        out_shape=jax.ShapeDtypeStruct((len(blocks) * share, blocks[0].shape[1]), jnp.bfloat16),
+        in_specs=[ANY] * len(blocks),
+        out_specs=VMEM,
+        scratch_shapes=[pltpu.SemaphoreType.DMA((len(blocks),))],
+        compiler_params=params(),
+        name="sibling",
+    )(*landed)
+    return [*landed, paired(sibling, 1)]
+
+
 def permuted(arrays, slopes, distance, gate_rows, head_dim, share):
-    (rows, width), count = arrays[0].shape, lax.axis_size("frame")
+    rows, count = arrays[0].shape[0], lax.axis_size("frame")
+    turns, width = count // 2, slopes.shape[0] * head_dim
     held = [pltpu.with_memory_space_constraint(value, pltpu.HBM) for value in arrays]
 
     def gathered(some):
         return pl.pallas_call(
             functools.partial(gather_kernel, some, share, width),
-            out_shape=[pltpu.VMEM((share, 3 * width), jnp.bfloat16) for _ in some],
+            out_shape=[pltpu.VMEM((2 * share, 3 * width), jnp.bfloat16) for _ in some],
             in_specs=[HBM] * 3,
             out_specs=[VMEM] * len(some),
             scratch_shapes=[pltpu.SemaphoreType.DMA((3 * len(some),))],
@@ -227,17 +271,14 @@
             name="gather",
         )(*held)
 
-    order = far_steps(count) + near_steps(count) + [0]
+    order = turn_order(count) + [0]
     blocks = dict(zip(order, [*gathered(order[:EARLY]), *gathered(order[EARLY:])]))
-    landed = []
-    for step in range(count):
-        block = paired(blocks[step], step) if step else blocks[step]
-        landed.append(pltpu.with_memory_space_constraint(block, pltpu.VMEM))
-    temporal = pl.pallas_call(
-        functools.partial(paired_kernel, count, head_dim, share),
-        out_shape=jax.ShapeDtypeStruct((rows, width), jnp.bfloat16),
-        in_specs=[SMEM, VMEM, VMEM] + [VMEM] * count,
-        out_specs=HBM,
+    landed = across_chips([blocks[turn] for turn in range(turns)], share)
+    outs = pl.pallas_call(
+        functools.partial(paired_kernel, turns, head_dim, share),
+        out_shape=[jax.ShapeDtypeStruct((2 * share, width), jnp.bfloat16) for _ in range(turns)],
+        in_specs=[SMEM, VMEM, VMEM] + [ANY] * (turns + 1),
+        out_specs=[VMEM] * turns,
         scratch_shapes=[
             pltpu.VMEM((rows, 3 * width), jnp.bfloat16),
             pltpu.VMEM((rows, width), jnp.bfloat16),
@@ -245,9 +286,18 @@
         ],
         cost_estimate=cost(rows, width, 4),
         compiler_params=params(),
-        name="temporal",
+        name="temporala",
     )(slopes, distance, gate_rows, *landed)
-    return lax.all_to_all(temporal, "frame", split_axis=0, concat_axis=0, tiled=True)
+    back = across_chips(outs, share)
+    return pl.pallas_call(
+        functools.partial(assemble_kernel, share),
+        out_shape=jax.ShapeDtypeStruct((rows, width), jnp.bfloat16),
+        in_specs=[ANY] * (turns + 1),
+        out_specs=VMEM,
+        scratch_shapes=[pltpu.SemaphoreType.DMA((count,))],
+        compiler_params=params(),
+        name="assemble",
+    )(*back)
 
 
 def body(queries, key_rows, value_rows, slopes, noise_level, frame_times):
@@ -260,10 +310,15 @@
     slopes = slopes.astype(jnp.float32)
     arrays = (queries, key_rows, value_rows)
     carried = spatial_part(*arrays, signal_gate, head_dim)
-    paired_up = in_pairs(frame_rows, count)
-    distance, gate_rows = tables(frame_times, noise_gate, paired_up, share, head_dim)
-    spread = permuted if paired_up else exchanged
-    temporal = spread(arrays, slopes, distance, gate_rows, head_dim, share)
+    distance, gate_rows = tables(frame_times, noise_gate, share, head_dim)
+    if in_pairs(frame_rows, count):
+        first = head_count * SPLIT[0] // SPLIT[1]
+        part_a = permuted(arrays, slopes[:first], distance, gate_rows, head_dim, share)
+        later = [value[:, first * head_dim :] for value in arrays]
+        part_b = exchanged(later, slopes[first:], distance, gate_rows, head_dim, share)
+        temporal = jnp.concatenate([part_a, part_b], axis=1)
+    else:
+        temporal = exchanged(arrays, slopes, distance, gate_rows, head_dim, share)
     return (carried.astype(jnp.float32) + temporal.astype(jnp.float32)).astype(jnp.bfloat16)
 
 

time: 75.6 us -> 82.3 us (1.089)
  the two profiles are of different devices: /device:TPU:13 before, /device:TPU:0 now
where the time goes in v1:
time: 82.3 us; the launch traced here: 81.8 us
  starting transfers between devices  39 us (47%)
  waiting for transfers between devices  28 us (34%)
  Pallas kernels  10.3 us (13%)
  other arithmetic  2.93 us (4%)
  local copies, waits for them, and re-layouts  1.27 us (2%)
    ppermute x16, waiting for transfers between devices, paired(): lax.ppermute(value, 'frame', [(device, device ^ step) for device in range...  28 us
    ppermute x16, starting transfers between devices, paired(): lax.ppermute(value, 'frame', [(device, device ^ step) for device in range...  23.5 us
    all_to_all x1, starting transfers between devices, exchanged(): lax.all_to_all(jnp.concatenate(arrays, axis=1), 'frame', split_axis=0, co...  7.41 us
    all_to_all x1, starting transfers between devices, exchanged(): lax.all_to_all(temporal, 'frame', split_axis=0, concat_axis=0, tiled=True)  6.83 us
    pallas_call x1, Pallas kernels, permuted(): pl.pallas_call(functools.partial(paired_kernel, turns, head_dim, share),...  3.01 us
    pallas_call x2, Pallas kernels, gathered(): pl.pallas_call(functools.partial(gather_kernel, some, share, width), out_...  2.2 us
    convert_element_type x1, other arithmetic, body(): (carried.astype(jnp.float32) + temporal.astype(jnp.float32)).astype(jnp.b...  1.96 us
    pallas_call x1, Pallas kernels, exchanged(): pl.pallas_call(functools.partial(plain_kernel, head_dim, share), out_shap...  1.79 us
  transfers between devices with their start and end apart: 19, of which 8 were waited for; matrix products, arithmetic and copies ran while one was open for 0% of the time, Pallas kernels for 13%

profile of v1, /device:TPU:0, one launch (start us, length us, event | category | flops | bytes accessed | tf_op | source)
XLA Modules:
  0.0 81.8 jit_solution(2509598694436345265)
XLA Ops:
  0.0 0.9 %slice-done = bf16[128,896]{1,0:T(8,128)(2,1)S(1)} async-done(((bf16[128,2048]{1,0:T(8,128)(2,1)}), bf16[128,896]{1,0:T(8,128)(2,1)S(1)}, s32[]{:S(2)}) %slice-start) | async-done | bytes 229400 | tf_op jit(solution)/shard_map/slice | solution.py:317
  1.2 0.9 %maximum_bitcast_fusion = bf16[16,8,2688]{2,1,0:T(8,128)(2,1)} fusion(bf16[128,896]{1,0:T(8,128)(2,1)S(1)} %slice-done.2, bf16[128,896]{1,0:T(8,128)(2,1)S(1)} %slice-done.1, bf16[128,896]{1,0:T(8,128)(2,1)S(1)} %slice-done), kind=kLoop, calls=%fused_computation.1 | loop fusion | flops 2064384 | bytes 1376256 | tf_op jit(solution)/shard_map/all_to_all | solution.py:225
  2.1 7.4 %all-to-all-start = ((bf16[16,8,2688]{2,1,0:T(8,128)(2,1)}), bf16[16,8,2688]{2,1,0:T(8,128)(2,1)S(1)}, u32[]{:S(2)}, u32[]{:S(2)}) async-start(bf16[16,8,2688]{2,1,0:T(8,128)(2,1)} %maximum_bitcast_fusion), calls=%async_computation | async-start | bytes 1376256 | tf_op jit(solution)/shard_map/all_to_all | solution.py:225
  9.5 1.2 %gather.2 = (bf16[16,3456]{1,0:T(8,128)(2,1)S(1)}, bf16[16,3456]{1,0:T(8,128)(2,1)S(1)}, bf16[16,3456]{1,0:T(8,128)(2,1)S(1)}, bf16[16,3456]{1,0:T(8,128)(2,1)S(...) custom-call(bf16[128,2048]{1,0:T(8,128)(2,1)} %query_ref.5, bf16[128,2048]{1,0:T(8,128)(2,1)} %key_ref.5, ...), custom_call_target="tpu_custom_call" | custom-call | tf_op jit(solution)/shard_map/gather/pallas_call | solution.py:264
  10.7 2.0 %collective-permute-start.1 = (bf16[16,3456]{1,0:T(8,128)(2,1)S(1)}, bf16[16,3456]{1,0:T(8,128)(2,1)S(1)}, u32[]{:S(2)}, u32[]{:S(2)}) collective-permute-start(bf16[16,3456]{1,0:T(8,128)(2,1)S(1)} %get-tuple-element.26), channel_id=1, source_target_pairs={{0,2},{1,3},{2,0},{3,1},{4,6},{5,7},{6,4},{7,5},{8,10},{9,11},{10,... | collective-permute-start | bytes 331784 | tf_op jit(solution)/shard_map/ppermute | solution.py:33
  12.7 1.5 %collective-permute-start.2 = (bf16[16,3456]{1,0:T(8,128)(2,1)S(1)}, bf16[16,3456]{1,0:T(8,128)(2,1)S(1)}, u32[]{:S(2)}, u32[]{:S(2)}) collective-permute-start(bf16[16,3456]{1,0:T(8,128)(2,1)S(1)} %get-tuple-element.27), channel_id=1, source_target_pairs={{0,4},{1,5},{2,6},{3,7},{4,0},{5,1},{6,2},{7,3},{8,12},{9,13},{10,... | collective-permute-start | bytes 331784 | tf_op jit(solution)/shard_map/ppermute | solution.py:33
  14.3 3.7 %collective-permute-start.5 = (bf16[16,3456]{1,0:T(8,128)(2,1)S(1)}, bf16[16,3456]{1,0:T(8,128)(2,1)S(1)}, u32[]{:S(2)}, u32[]{:S(2)}) collective-permute-start(bf16[16,3456]{1,0:T(8,128)(2,1)S(1)} %get-tuple-element.30), channel_id=1, source_target_pairs={{0,10},{1,11},{2,8},{3,9},{4,14},{5,15},{6,12},{7,13},{8,2},{9,3},... | collective-permute-start | bytes 331784 | tf_op jit(solution)/shard_map/ppermute | solution.py:33
  18.0 1.5 %collective-permute-start.7 = (bf16[16,3456]{1,0:T(8,128)(2,1)S(1)}, bf16[16,3456]{1,0:T(8,128)(2,1)S(1)}, u32[]{:S(2)}, u32[]{:S(2)}) collective-permute-start(bf16[16,3456]{1,0:T(8,128)(2,1)S(1)} %get-tuple-element.32), channel_id=1, source_target_pairs={{0,14},{1,15},{2,12},{3,13},{4,10},{5,11},{6,8},{7,9},{8,6},{9,7},... | collective-permute-start | bytes 331784 | tf_op jit(solution)/shard_map/ppermute | solution.py:33
  19.5 1.0 %gather.3 = (bf16[16,3456]{1,0:T(8,128)(2,1)S(1)}, bf16[16,3456]{1,0:T(8,128)(2,1)S(1)}) custom-call(bf16[128,2048]{1,0:T(8,128)(2,1)} %query_ref.5, bf16[128,2048]{1,0:T(8,128)(2,1)} %key_ref.5, bf16[128,2048]{1,0:T(8,128)(2,1)} %value_ref.5), custom_call_target="tpu_custom_call" | custom-call | tf_op jit(solution)/shard_map/gather/pallas_call | solution.py:264
  20.5 1.5 %collective-permute-start.4 = (bf16[16,3456]{1,0:T(8,128)(2,1)S(1)}, bf16[16,3456]{1,0:T(8,128)(2,1)S(1)}, u32[]{:S(2)}, u32[]{:S(2)}) collective-permute-start(bf16[16,3456]{1,0:T(8,128)(2,1)S(1)} %get-tuple-element.29), channel_id=1, source_target_pairs={{0,8},{1,9},{2,10},{3,11},{4,12},{5,13},{6,14},{7,15},{8,0},{9,1},... | collective-permute-start | bytes 331784 | tf_op jit(solution)/shard_map/ppermute | solution.py:33
  22.0 4.1 %collective-permute-done.2.refs_2_.rest_2_ = bf16[16,3456]{1,0:T(8,128)(2,1)S(1)} collective-permute-done((bf16[16,3456]{1,0:T(8,128)(2,1)S(1)}, bf16[16,3456]{1,0:T(8,128)(2,1)S(1)}, u32[]{:S(2)}, u32[]{:S(2)}) %collective-permute-start.2) | collective-permute-done | bytes 110624 | tf_op jit(solution)/shard_map/ppermute | solution.py:33
  26.2 1.9 %collective-permute-start.6 = (bf16[16,3456]{1,0:T(8,128)(2,1)S(1)}, bf16[16,3456]{1,0:T(8,128)(2,1)S(1)}, u32[]{:S(2)}, u32[]{:S(2)}) collective-permute-start(bf16[16,3456]{1,0:T(8,128)(2,1)S(1)} %get-tuple-element.31), channel_id=1, source_target_pairs={{0,12},{1,13},{2,14},{3,15},{4,8},{5,9},{6,10},{7,11},{8,4},{9,5},... | collective-permute-start | bytes 331784 | tf_op jit(solution)/shard_map/ppermute | solution.py:33
  28.1 2.8 %collective-permute-done.3.refs_3_.rest_3_ = bf16[16,3456]{1,0:T(8,128)(2,1)S(1)} collective-permute-done((bf16[16,3456]{1,0:T(8,128)(2,1)S(1)}, bf16[16,3456]{1,0:T(8,128)(2,1)S(1)}, u32[]{:S(2)}, u32[]{:S(2)}) %collective-permute-start.3) | collective-permute-done | bytes 110624 | tf_op jit(solution)/shard_map/ppermute | solution.py:33
  30.9 10.7 %collective-permute-done.5.refs_5_.rest_5_ = bf16[16,3456]{1,0:T(8,128)(2,1)S(1)} collective-permute-done((bf16[16,3456]{1,0:T(8,128)(2,1)S(1)}, bf16[16,3456]{1,0:T(8,128)(2,1)S(1)}, u32[]{:S(2)}, u32[]{:S(2)}) %collective-permute-start.5) | collective-permute-done | bytes 110624 | tf_op jit(solution)/shard_map/ppermute | solution.py:33
  41.6 3.8 %collective-permute-done.4.refs_4_.rest_4_ = bf16[16,3456]{1,0:T(8,128)(2,1)S(1)} collective-permute-done((bf16[16,3456]{1,0:T(8,128)(2,1)S(1)}, bf16[16,3456]{1,0:T(8,128)(2,1)S(1)}, u32[]{:S(2)}, u32[]{:S(2)}) %collective-permute-start.4) | collective-permute-done | bytes 110624 | tf_op jit(solution)/shard_map/ppermute | solution.py:33
  45.5 0.6 sibling.2
  46.3 1.4 %spatial.1 = bf16[128,2048]{1,0:T(8,128)(2,1)S(1)} custom-call(f32[16]{0:T(128)S(1)} %get-tuple-element.42.gate_ref, bf16[128,2048]{1,0:T(8,128)(2,1)S(1)} %copy-done, bf16[128,2048]{1,0:T(8,128)(2,1)S(1)} %copy-done.1, bf16[128,2048]{1,0:T(8,128)(2,1)S(1)} %copy-done.2), custom_call_target="tpu_custom_call" | custom-call | flops 134217728 | bytes 2097152 | tf_op jit(solution)/shard_map/spatial/pallas_call | solution.py:211
  47.7 1.3 %collective-permute-start = (bf16[128,2048]{1,0:T(8,128)(2,1)S(1)}, bf16[128,2048]{1,0:T(8,128)(2,1)}, u32[]{:S(2)}, u32[]{:S(2)}) collective-permute-start(bf16[128,2048]{1,0:T(8,128)(2,1)S(1)} %spatial.1), channel_id=1, source_target_pairs={{1,0},{2,1},{3,2},{4,3},{5,4},{6,5},{7,6},{8,7},{9,8},{10,9},{11,1... | collective-permute-start | bytes 1572872 | tf_op jit(solution)/shard_map/ppermute | solution.py:28
  49.0 0.6 tables.1
  49.6 1.8 %temporalb.1 = bf16[128,896]{1,0:T(8,128)(2,1)} custom-call(f32[7]{0:T(128)S(1)} %slice.16.slopes_ref, f32[128,128]{1,0:T(8,128)S(1)} %get-tuple-element.23.distance_ref, f32[128,128]{1,0:T(8,128)S(1)} %get-tuple-element.24.gate_ref, bf16[128,2688]{1,0:T(8,128)(2,1)S(1)} %bitcast.5), custom_call_target="tpu_custom_call" | custom-call | flops 58720256 | bytes 917504 | tf_op jit(solution)/shard_map/temporalb/pallas_call | solution.py:226
  51.4 6.8 %all-to-all-start.1 = ((bf16[16,8,896]{2,1,0:T(8,128)(2,1)}), bf16[16,8,896]{2,1,0:T(8,128)(2,1)S(1)}, u32[]{:S(2)}, u32[]{:S(2)}) async-start(bf16[16,8,896]{2,1,0:T(8,128)(2,1)} %bitcast.2), calls=%async_computation.1 | async-start | bytes 458752 | tf_op jit(solution)/shard_map/all_to_all | solution.py:235
  58.3 3.0 %temporala.1 = (bf16[16,1152]{1,0:T(8,128)(2,1)S(1)}, bf16[16,1152]{1,0:T(8,128)(2,1)S(1)}, bf16[16,1152]{1,0:T(8,128)(2,1)S(1)}, bf16[16,1152]{1,0:T(8,128)(2,1...) custom-call(f32[9]{0:T(128)S(1)} %slice.15.slopes_ref, ...), custom_call_target="tpu_custom_call" | custom-call | flops 75497472 | bytes 1179648 | tf_op jit(solution)/shard_map/temporala/pallas_call | solution.py:277
  61.3 2.0 %collective-permute-start.10 = (bf16[16,1152]{1,0:T(8,128)(2,1)S(1)}, bf16[16,1152]{1,0:T(8,128)(2,1)S(1)}, u32[]{:S(2)}, u32[]{:S(2)}) collective-permute-start(bf16[16,1152]{1,0:T(8,128)(2,1)S(1)} %get-tuple-element.35), channel_id=1, source_target_pairs={{0,4},{1,5},{2,6},{3,7},{4,0},{5,1},{6,2},{7,3},{8,12},{9,13},{10,... | collective-permute-start | bytes 110600 | tf_op jit(solution)/shard_map/ppermute | solution.py:33
  63.3 1.5 %collective-permute-start.11 = (bf16[16,1152]{1,0:T(8,128)(2,1)S(1)}, bf16[16,1152]{1,0:T(8,128)(2,1)S(1)}, u32[]{:S(2)}, u32[]{:S(2)}) collective-permute-start(bf16[16,1152]{1,0:T(8,128)(2,1)S(1)} %get-tuple-element.36), channel_id=1, source_target_pairs={{0,6},{1,7},{2,4},{3,5},{4,2},{5,3},{6,0},{7,1},{8,14},{9,15},{10,... | collective-permute-start | bytes 110600 | tf_op jit(solution)/shard_map/ppermute | solution.py:33
  64.7 2.4 %collective-permute-start.12 = (bf16[16,1152]{1,0:T(8,128)(2,1)S(1)}, bf16[16,1152]{1,0:T(8,128)(2,1)S(1)}, u32[]{:S(2)}, u32[]{:S(2)}) collective-permute-start(bf16[16,1152]{1,0:T(8,128)(2,1)S(1)} %get-tuple-element.37), channel_id=1, source_target_pairs={{0,8},{1,9},{2,10},{3,11},{4,12},{5,13},{6,14},{7,15},{8,0},{9,1},... | collective-permute-start | bytes 110600 | tf_op jit(solution)/shard_map/ppermute | solution.py:33
  67.2 3.7 %collective-permute-start.14 = (bf16[16,1152]{1,0:T(8,128)(2,1)S(1)}, bf16[16,1152]{1,0:T(8,128)(2,1)S(1)}, u32[]{:S(2)}, u32[]{:S(2)}) collective-permute-start(bf16[16,1152]{1,0:T(8,128)(2,1)S(1)} %get-tuple-element.39), channel_id=1, source_target_pairs={{0,12},{1,13},{2,14},{3,15},{4,8},{5,9},{6,10},{7,11},{8,4},{9,5},... | collective-permute-start | bytes 110600 | tf_op jit(solution)/shard_map/ppermute | solution.py:33
  70.9 1.5 %collective-permute-start.15 = (bf16[16,1152]{1,0:T(8,128)(2,1)S(1)}, bf16[16,1152]{1,0:T(8,128)(2,1)S(1)}, u32[]{:S(2)}, u32[]{:S(2)}) collective-permute-start(bf16[16,1152]{1,0:T(8,128)(2,1)S(1)} %get-tuple-element.40), channel_id=1, source_target_pairs={{0,14},{1,15},{2,12},{3,13},{4,10},{5,11},{6,8},{7,9},{8,6},{9,7},... | collective-permute-start | bytes 110600 | tf_op jit(solution)/shard_map/ppermute | solution.py:33
  72.5 0.7 collective-permute-done.13.refs_5_
  73.3 4.2 %collective-permute-done.15.refs_7_ = bf16[16,1152]{1,0:T(8,128)(2,1)S(1)} collective-permute-done((bf16[16,1152]{1,0:T(8,128)(2,1)S(1)}, bf16[16,1152]{1,0:T(8,128)(2,1)S(1)}, u32[]{:S(2)}, u32[]{:S(2)}) %collective-permute-start.15) | collective-permute-done | bytes 36896 | tf_op jit(solution)/shard_map/ppermute | solution.py:33
  77.9 1.4 %collective-permute-done.16.refs_8_ = bf16[64,1152]{1,0:T(8,128)(2,1)S(1)} collective-permute-done((bf16[64,1152]{1,0:T(8,128)(2,1)S(1)}, bf16[64,1152]{1,0:T(8,128)(2,1)S(1)}, u32[]{:S(2)}, u32[]{:S(2)}) %collective-permute-start.16) | collective-permute-done | bytes 147488 | tf_op jit(solution)/shard_map/ppermute | solution.py:33
  79.3 0.5 assemble.1
  79.8 2.0 %add_convert_fusion = bf16[128,2048]{1,0:T(8,128)(2,1)} fusion(bf16[128,2048]{1,0:T(8,128)(2,1)} %collective-permute-done, bf16[128,896]{1,0:T(8,128)(2,1)S(1)} %bitcast.6, bf16[128,1152]{1,0:T(8,128)(2,1)S(1)} %assemble.1), kind=kLoop, calls=%fused_computation | loop fusion | flops 1835008 | bytes 1572864 | tf_op jit(solution)/shard_map/convert_element_type | solution.py:322
  (38 shorter events, 1.2 us)
Async XLA Ops:
  0.0 0.9 %slice-start = ((bf16[128,2048]{1,0:T(8,128)(2,1)}), bf16[128,896]{1,0:T(8,128)(2,1)S(1)}, s32[]{:S(2)}) async-start(bf16[128,2048]{1,0:T(8,128)(2,1)} %query_ref.5), calls=%async_computation.2 | async-start | bytes 458752 | tf_op jit(solution)/shard_map/slice | solution.py:317
  0.0 1.0 %slice-start.1 = ((bf16[128,2048]{1,0:T(8,128)(2,1)}), bf16[128,896]{1,0:T(8,128)(2,1)S(1)}, s32[]{:S(2)}) async-start(bf16[128,2048]{1,0:T(8,128)(2,1)} %key_ref.5), calls=%async_computation.3 | async-start | bytes 458752 | tf_op jit(solution)/shard_map/slice | solution.py:317
  0.0 1.2 %slice-start.2 = ((bf16[128,2048]{1,0:T(8,128)(2,1)}), bf16[128,896]{1,0:T(8,128)(2,1)S(1)}, s32[]{:S(2)}) async-start(bf16[128,2048]{1,0:T(8,128)(2,1)} %value_ref.5), calls=%async_computation.4 | async-start | bytes 458752 | tf_op jit(solution)/shard_map/slice | solution.py:317
  2.1 47.5 %all-to-all-start = ((bf16[16,8,2688]{2,1,0:T(8,128)(2,1)}), bf16[16,8,2688]{2,1,0:T(8,128)(2,1)S(1)}, u32[]{:S(2)}, u32[]{:S(2)}) async-start(bf16[16,8,2688]{2,1,0:T(8,128)(2,1)} %maximum_bitcast_fusion), calls=%async_computation | async-start | bytes 1376256 | tf_op jit(solution)/shard_map/all_to_all | solution.py:225
  10.7 9.7 %collective-permute-start.1 = (bf16[16,3456]{1,0:T(8,128)(2,1)S(1)}, bf16[16,3456]{1,0:T(8,128)(2,1)S(1)}, u32[]{:S(2)}, u32[]{:S(2)}) collective-permute-start(bf16[16,3456]{1,0:T(8,128)(2,1)S(1)} %get-tuple-element.26), channel_id=1, source_target_pairs={{0,2},{1,3},{2,0},{3,1},{4,6},{5,7},{6,4},{7,5},{8,10},{9,11},{10,... | collective-permute-start | bytes 331784 | tf_op jit(solution)/shard_map/ppermute | solution.py:33
  12.7 13.5 %collective-permute-start.2 = (bf16[16,3456]{1,0:T(8,128)(2,1)S(1)}, bf16[16,3456]{1,0:T(8,128)(2,1)S(1)}, u32[]{:S(2)}, u32[]{:S(2)}) collective-permute-start(bf16[16,3456]{1,0:T(8,128)(2,1)S(1)} %get-tuple-element.27), channel_id=1, source_target_pairs={{0,4},{1,5},{2,6},{3,7},{4,0},{5,1},{6,2},{7,3},{8,12},{9,13},{10,... | collective-permute-start | bytes 331784 | tf_op jit(solution)/shard_map/ppermute | solution.py:33
  14.2 16.7 %collective-permute-start.3 = (bf16[16,3456]{1,0:T(8,128)(2,1)S(1)}, bf16[16,3456]{1,0:T(8,128)(2,1)S(1)}, u32[]{:S(2)}, u32[]{:S(2)}) collective-permute-start(bf16[16,3456]{1,0:T(8,128)(2,1)S(1)} %get-tuple-element.28), channel_id=1, source_target_pairs={{0,6},{1,7},{2,4},{3,5},{4,2},{5,3},{6,0},{7,1},{8,14},{9,15},{10,... | collective-permute-start | bytes 331784 | tf_op jit(solution)/shard_map/ppermute | solution.py:33
  14.3 27.4 %collective-permute-start.5 = (bf16[16,3456]{1,0:T(8,128)(2,1)S(1)}, bf16[16,3456]{1,0:T(8,128)(2,1)S(1)}, u32[]{:S(2)}, u32[]{:S(2)}) collective-permute-start(bf16[16,3456]{1,0:T(8,128)(2,1)S(1)} %get-tuple-element.30), channel_id=1, source_target_pairs={{0,10},{1,11},{2,8},{3,9},{4,14},{5,15},{6,12},{7,13},{8,2},{9,3},... | collective-permute-start | bytes 331784 | tf_op jit(solution)/shard_map/ppermute | solution.py:33
  18.0 23.6 %collective-permute-start.7 = (bf16[16,3456]{1,0:T(8,128)(2,1)S(1)}, bf16[16,3456]{1,0:T(8,128)(2,1)S(1)}, u32[]{:S(2)}, u32[]{:S(2)}) collective-permute-start(bf16[16,3456]{1,0:T(8,128)(2,1)S(1)} %get-tuple-element.32), channel_id=1, source_target_pairs={{0,14},{1,15},{2,12},{3,13},{4,10},{5,11},{6,8},{7,9},{8,6},{9,7},... | collective-permute-start | bytes 331784 | tf_op jit(solution)/shard_map/ppermute | solution.py:33
  19.5 26.8 %copy-start.2 = (bf16[128,2048]{1,0:T(8,128)(2,1)S(1)}, bf16[128,2048]{1,0:T(8,128)(2,1)}, u32[]{:S(2)}) copy-start(bf16[128,2048]{1,0:T(8,128)(2,1)} %value_ref.5) | copy-start | bytes 1572868
  20.4 25.7 %copy-start.4 = (s32[16]{0:T(128)S(1)}, s32[16]{0:T(128)}, u32[]{:S(2)}) copy-start(s32[16]{0:T(128)} %param.10) | copy-start | bytes 196
  20.5 25.8 %copy-start = (bf16[128,2048]{1,0:T(8,128)(2,1)S(1)}, bf16[128,2048]{1,0:T(8,128)(2,1)}, u32[]{:S(2)}) copy-start(bf16[128,2048]{1,0:T(8,128)(2,1)} %query_ref.5) | copy-start | bytes 1572868
  20.5 25.8 %copy-start.1 = (bf16[128,2048]{1,0:T(8,128)(2,1)S(1)}, bf16[128,2048]{1,0:T(8,128)(2,1)}, u32[]{:S(2)}) copy-start(bf16[128,2048]{1,0:T(8,128)(2,1)} %key_ref.5) | copy-start | bytes 1572868
  20.5 25.0 %collective-permute-start.4 = (bf16[16,3456]{1,0:T(8,128)(2,1)S(1)}, bf16[16,3456]{1,0:T(8,128)(2,1)S(1)}, u32[]{:S(2)}, u32[]{:S(2)}) collective-permute-start(bf16[16,3456]{1,0:T(8,128)(2,1)S(1)} %get-tuple-element.29), channel_id=1, source_target_pairs={{0,8},{1,9},{2,10},{3,11},{4,12},{5,13},{6,14},{7,15},{8,0},{9,1},... | collective-permute-start | bytes 331784 | tf_op jit(solution)/shard_map/ppermute | solution.py:33
  26.2 19.3 %collective-permute-start.6 = (bf16[16,3456]{1,0:T(8,128)(2,1)S(1)}, bf16[16,3456]{1,0:T(8,128)(2,1)S(1)}, u32[]{:S(2)}, u32[]{:S(2)}) collective-permute-start(bf16[16,3456]{1,0:T(8,128)(2,1)S(1)} %get-tuple-element.31), channel_id=1, source_target_pairs={{0,12},{1,13},{2,14},{3,15},{4,8},{5,9},{6,10},{7,11},{8,4},{9,5},... | collective-permute-start | bytes 331784 | tf_op jit(solution)/shard_map/ppermute | solution.py:33
  46.1 12.2 %collective-permute-start.8 = (bf16[64,3456]{1,0:T(8,128)(2,1)S(1)}, bf16[64,3456]{1,0:T(8,128)(2,1)S(1)}, u32[]{:S(2)}, u32[]{:S(2)}) collective-permute-start(bf16[64,3456]{1,0:T(8,128)(2,1)S(1)} %sibling.2), channel_id=1, source_target_pairs={{0,1},{1,0},{2,3},{3,2},{4,5},{5,4},{6,7},{7,6},{8,9},{9,8},{10,11... | collective-permute-start | bytes 1327112 | tf_op jit(solution)/shard_map/ppermute | solution.py:33
  46.3 2.7 %copy-start.5 = (bf16[16]{0:T(256)(128)(2,1)S(1)}, bf16[16]{0:T(256)(128)(2,1)}, u32[]{:S(2)}) copy-start(bf16[16]{0:T(256)(128)(2,1)} %param.9) | copy-start | bytes 100
  46.3 2.8 %copy-start.3 = (s32[16]{0:T(128)S(1)}, s32[16]{0:T(128)}, u32[]{:S(2)}) copy-start(s32[16]{0:T(128)} %times_ref.1) | copy-start | bytes 196
  47.7 32.2 %collective-permute-start = (bf16[128,2048]{1,0:T(8,128)(2,1)S(1)}, bf16[128,2048]{1,0:T(8,128)(2,1)}, u32[]{:S(2)}, u32[]{:S(2)}) collective-permute-start(bf16[128,2048]{1,0:T(8,128)(2,1)S(1)} %spatial.1), channel_id=1, source_target_pairs={{1,0},{2,1},{3,2},{4,3},{5,4},{6,5},{7,6},{8,7},{9,8},{10,9},{11,1... | collective-permute-start | bytes 1572872 | tf_op jit(solution)/shard_map/ppermute | solution.py:28
  51.4 28.4 %all-to-all-start.1 = ((bf16[16,8,896]{2,1,0:T(8,128)(2,1)}), bf16[16,8,896]{2,1,0:T(8,128)(2,1)S(1)}, u32[]{:S(2)}, u32[]{:S(2)}) async-start(bf16[16,8,896]{2,1,0:T(8,128)(2,1)} %bitcast.2), calls=%async_computation.1 | async-start | bytes 458752 | tf_op jit(solution)/shard_map/all_to_all | solution.py:235
  61.3 5.9 %collective-permute-start.10 = (bf16[16,1152]{1,0:T(8,128)(2,1)S(1)}, bf16[16,1152]{1,0:T(8,128)(2,1)S(1)}, u32[]{:S(2)}, u32[]{:S(2)}) collective-permute-start(bf16[16,1152]{1,0:T(8,128)(2,1)S(1)} %get-tuple-element.35), channel_id=1, source_target_pairs={{0,4},{1,5},{2,6},{3,7},{4,0},{5,1},{6,2},{7,3},{8,12},{9,13},{10,... | collective-permute-start | bytes 110600 | tf_op jit(solution)/shard_map/ppermute | solution.py:33
  63.3 7.7 %collective-permute-start.11 = (bf16[16,1152]{1,0:T(8,128)(2,1)S(1)}, bf16[16,1152]{1,0:T(8,128)(2,1)S(1)}, u32[]{:S(2)}, u32[]{:S(2)}) collective-permute-start(bf16[16,1152]{1,0:T(8,128)(2,1)S(1)} %get-tuple-element.36), channel_id=1, source_target_pairs={{0,6},{1,7},{2,4},{3,5},{4,2},{5,3},{6,0},{7,1},{8,14},{9,15},{10,... | collective-permute-start | bytes 110600 | tf_op jit(solution)/shard_map/ppermute | solution.py:33
  64.7 7.7 %collective-permute-start.12 = (bf16[16,1152]{1,0:T(8,128)(2,1)S(1)}, bf16[16,1152]{1,0:T(8,128)(2,1)S(1)}, u32[]{:S(2)}, u32[]{:S(2)}) collective-permute-start(bf16[16,1152]{1,0:T(8,128)(2,1)S(1)} %get-tuple-element.37), channel_id=1, source_target_pairs={{0,8},{1,9},{2,10},{3,11},{4,12},{5,13},{6,14},{7,15},{8,0},{9,1},... | collective-permute-start | bytes 110600 | tf_op jit(solution)/shard_map/ppermute | solution.py:33
  67.1 6.1 %collective-permute-start.13 = (bf16[16,1152]{1,0:T(8,128)(2,1)S(1)}, bf16[16,1152]{1,0:T(8,128)(2,1)S(1)}, u32[]{:S(2)}, u32[]{:S(2)}) collective-permute-start(bf16[16,1152]{1,0:T(8,128)(2,1)S(1)} %get-tuple-element.38), channel_id=1, source_target_pairs={{0,10},{1,11},{2,8},{3,9},{4,14},{5,15},{6,12},{7,13},{8,2},{9,3},... | collective-permute-start | bytes 110600 | tf_op jit(solution)/shard_map/ppermute | solution.py:33
  67.2 6.1 %collective-permute-start.14 = (bf16[16,1152]{1,0:T(8,128)(2,1)S(1)}, bf16[16,1152]{1,0:T(8,128)(2,1)S(1)}, u32[]{:S(2)}, u32[]{:S(2)}) collective-permute-start(bf16[16,1152]{1,0:T(8,128)(2,1)S(1)} %get-tuple-element.39), channel_id=1, source_target_pairs={{0,12},{1,13},{2,14},{3,15},{4,8},{5,9},{6,10},{7,11},{8,4},{9,5},... | collective-permute-start | bytes 110600 | tf_op jit(solution)/shard_map/ppermute | solution.py:33
  70.9 6.7 %collective-permute-start.15 = (bf16[16,1152]{1,0:T(8,128)(2,1)S(1)}, bf16[16,1152]{1,0:T(8,128)(2,1)S(1)}, u32[]{:S(2)}, u32[]{:S(2)}) collective-permute-start(bf16[16,1152]{1,0:T(8,128)(2,1)S(1)} %get-tuple-element.40), channel_id=1, source_target_pairs={{0,14},{1,15},{2,12},{3,13},{4,10},{5,11},{6,8},{7,9},{8,6},{9,7},... | collective-permute-start | bytes 110600 | tf_op jit(solution)/shard_map/ppermute | solution.py:33
  72.4 5.2 %collective-permute-start.9 = (bf16[16,1152]{1,0:T(8,128)(2,1)S(1)}, bf16[16,1152]{1,0:T(8,128)(2,1)S(1)}, u32[]{:S(2)}, u32[]{:S(2)}) collective-permute-start(bf16[16,1152]{1,0:T(8,128)(2,1)S(1)} %get-tuple-element.34), channel_id=1, source_target_pairs={{0,2},{1,3},{2,0},{3,1},{4,6},{5,7},{6,4},{7,5},{8,10},{9,11},{10,... | collective-permute-start | bytes 110600 | tf_op jit(solution)/shard_map/ppermute | solution.py:33
  77.8 1.4 %collective-permute-start.16 = (bf16[64,1152]{1,0:T(8,128)(2,1)S(1)}, bf16[64,1152]{1,0:T(8,128)(2,1)S(1)}, u32[]{:S(2)}, u32[]{:S(2)}) collective-permute-start(bf16[64,1152]{1,0:T(8,128)(2,1)S(1)} %sibling.3), channel_id=1, source_target_pairs={{0,1},{1,0},{2,3},{3,2},{4,5},{5,4},{6,7},{7,6},{8,9},{9,8},{10,11... | collective-permute-start | bytes 442376 | tf_op jit(solution)/shard_map/ppermute | solution.py:33
